TPU v7x, 256 devices: a whole 4x4x8 slice. The times are simulated.
256 devices in a mesh: dp: 16 (over x, y), tensor: 16 (over z, core).
Axes of the slice: x: 4, y: 4, z: 8, core: 2. Of those that a mesh axis runs over, the one named last changes fastest.
Arguments:
- tokens: bfloat16 [8192, 8192], P(('dp', 'tensor')), may hold values from -6 to 6
- w_query: bfloat16 [8192, 8192], P(None, 'tensor'), may hold values from -0.0625 to 0.0625
- cotangent: bfloat16 [8192, 8192], P('dp', 'tensor'), may hold values from -6 to 6
- task_embed: bfloat16 [128, 1024], replicated, may hold values from -6 to 6
- w_hidden: bfloat16 [1024, 512], P(None, 'tensor'), may hold values from -0.1875 to 0.1875
- head_a: bfloat16 [512, 16, 8192], P(None, 'dp', 'tensor'), may hold values from -0.0234375 to 0.0234375
- head_b: bfloat16 [512, 16, 8192], P(None, 'dp', 'tensor'), may hold values from -0.0234375 to 0.0234375
- block_task: int32 [16], replicated, may hold values from 0 to 127
Outputs:
- output: bfloat16 [8192, 8192], P('dp', 'tensor')
- grad_tokens: bfloat16 [8192, 8192], P(('dp', 'tensor'))
- grad_head_a: bfloat16 [512, 16, 8192], P(None, 'dp', 'tensor')
- grad_head_b: bfloat16 [512, 16, 8192], P(None, 'dp', 'tensor')
All inputs are finite; a program needn't handle non-finite values.
Results may differ from a plain program's by a relative error of at most 0.0077.
Values may be sent and summed in bfloat16 or wider, within the bound.
No kernel may reach another device: no remote copies, remote signals or barrier semaphores. Data moves between devices by JAX's collectives and lax.ppermute only.
A program may use at most 128 MiB of HBM per device.

v0:
```python
import jax
import jax.numpy as jnp
from jax import lax
from jax.sharding import PartitionSpec as P


def local(tokens, w_query, cotangent, task_embed, w_hidden, head_a, head_b, block_task):
    single_float = jnp.float32
    brain_half_float = jnp.bfloat16
    n_groups = lax.axis_size("dp")
    n_shards = lax.axis_size("tensor")
    shard = lax.axis_index("tensor")
    group = lax.axis_index("dp")
    hid_count, rank_rows, width = head_a.shape
    ntasks = task_embed.shape[0]
    blocks = block_task.shape[0]
    per_group = blocks // n_groups
    hid_part = jax.nn.silu(
        jnp.dot(task_embed, w_hidden, preferred_element_type=single_float)
    ).astype(brain_half_float)
    hidden = lax.all_gather(hid_part, "tensor", axis=1, tiled=True)
    flat_a = head_a.reshape(hid_count, rank_rows * width)
    flat_b = head_b.reshape(hid_count, rank_rows * width)
    mine = lax.dynamic_slice_in_dim(block_task, group * per_group, per_group)
    task_ids = jnp.arange(ntasks, dtype=jnp.int32)
    gen_a = (
        jnp.dot(hidden, flat_a, preferred_element_type=single_float)
        .astype(brain_half_float)
        .reshape(ntasks, rank_rows, width)
    )
    gen_b = (
        jnp.dot(hidden, flat_b, preferred_element_type=single_float)
        .astype(brain_half_float)
        .reshape(ntasks, rank_rows, width)
    )
    all_tasks_down, all_tasks_up = (
        lax.all_gather(gen_a, "dp", axis=1, tiled=True),
        lax.all_gather(gen_b, "dp", axis=1, tiled=True),
    )
    task_selector = (mine[:, None] == task_ids[None, :]).astype(brain_half_float)
    adapter_down_weight = jnp.einsum(
        "yg,ghi->yhi", task_selector, all_tasks_down, preferred_element_type=single_float
    ).astype(brain_half_float)
    adapter_up_weight = jnp.einsum(
        "yg,ghi->yhi", task_selector, all_tasks_up, preferred_element_type=single_float
    ).astype(brain_half_float)
    rank = adapter_down_weight.shape[1]
    whole = lax.all_gather(tokens, "tensor", axis=0, tiled=True)
    rows_all, model_width = whole.shape
    block = rows_all // per_group
    rows_dev = rows_all // n_shards
    block_inputs = whole.reshape(per_group, block, model_width)
    input_columns = lax.dynamic_slice_in_dim(block_inputs, shard * width, width, 2)
    frozen_output = jnp.dot(whole, w_query, preferred_element_type=single_float)
    down_portion = jnp.einsum(
        "grs,gps->grp", input_columns, adapter_down_weight, preferred_element_type=single_float
    )
    down_projection = lax.psum(down_portion, "tensor")
    down_low_rank = down_projection.astype(brain_half_float)
    low_rank_update = jnp.einsum(
        "elm,emn->eln", down_low_rank, adapter_up_weight, preferred_element_type=single_float
    ).reshape(rows_all, width)
    output = (frozen_output + low_rank_update).astype(brain_half_float)
    block_output_grads = cotangent.reshape(per_group, block, width)
    backward_portion = jnp.einsum(
        "grs,gps->grp", block_output_grads, adapter_up_weight, preferred_element_type=single_float
    )
    backward_input = lax.psum(backward_portion, "tensor")
    backward_low_rank = backward_input.astype(brain_half_float)
    grad_sum = lax.psum_scatter(
        lax.dot_general(
            cotangent, w_query, (((1,), (1,)), ((), ())), preferred_element_type=single_float
        ),
        "tensor",
        scatter_dimension=0,
        tiled=True,
    )
    full_a = lax.all_gather(adapter_down_weight, "tensor", axis=2, tiled=True)
    first = shard * rows_dev
    which = first // block
    a_here = lax.dynamic_index_in_dim(full_a, which, 0, keepdims=False)
    back_rows = lax.dynamic_slice_in_dim(
        backward_low_rank.reshape(rows_all, rank), first, rows_dev, 0
    )
    grad_sum = grad_sum + jnp.dot(back_rows, a_here, preferred_element_type=single_float)
    grad_tokens = grad_sum.astype(brain_half_float)
    scale_average = 1.0 / block
    down_gradient = (
        jnp.einsum(
            "evr,evx->erx", backward_low_rank, input_columns, preferred_element_type=single_float
        )
        * scale_average
    ).astype(brain_half_float)
    up_gradient = (
        jnp.einsum(
            "evr,evx->erx", down_low_rank, block_output_grads, preferred_element_type=single_float
        )
        * scale_average
    ).astype(brain_half_float)
    task_down_weight = jnp.einsum(
        "xh,xui->hui", task_selector, down_gradient, preferred_element_type=single_float
    )
    task_up_weight = jnp.einsum(
        "xh,xui->hui", task_selector, up_gradient, preferred_element_type=single_float
    )
    own_a, own_b = (
        lax.psum_scatter(
            task_down_weight.astype(jnp.bfloat16), "dp", scatter_dimension=1, tiled=True
        ).astype(jnp.float32),
        lax.psum_scatter(
            task_up_weight.astype(jnp.bfloat16), "dp", scatter_dimension=1, tiled=True
        ).astype(jnp.float32),
    )
    hid_f = hidden.astype(single_float)
    head_grad_a = lax.dot_general(
        hid_f,
        own_a.reshape(ntasks, rank_rows * width),
        (((0,), (0,)), ((), ())),
        precision=lax.Precision.HIGHEST,
    )
    head_grad_b = lax.dot_general(
        hid_f,
        own_b.reshape(ntasks, rank_rows * width),
        (((0,), (0,)), ((), ())),
        precision=lax.Precision.HIGHEST,
    )
    grad_head_a = head_grad_a.reshape(hid_count, rank_rows, width).astype(brain_half_float)
    grad_head_b = head_grad_b.reshape(hid_count, rank_rows, width).astype(brain_half_float)
    return (output, grad_tokens, grad_head_a, grad_head_b)


def solution(mesh):
    return jax.shard_map(
        local,
        mesh=mesh,
        in_specs=(
            P(("dp", "tensor"), None),
            P(None, "tensor"),
            P("dp", "tensor"),
            P(),
            P(None, "tensor"),
            P(None, "dp", "tensor"),
            P(None, "dp", "tensor"),
            P(),
        ),
        out_specs=(
            P("dp", "tensor"),
            P(("dp", "tensor"), None),
            P(None, "dp", "tensor"),
            P(None, "dp", "tensor"),
        ),
        check_vma=False,
    )
```

profile of v0, /device:TPU:2, one launch (start us, length us, event | category | flops | bytes accessed | tf_op | source)
XLA Modules:
  0.0 520.4 jit_solution(2591239751184445774)
XLA Ops:
  7.2 1.2 multiply_convert_fusion.2
  8.4 20.3 %all_gather.16 = bf16[128,512]{0,1:T(8,128)(2,1)S(1)} all-gather(bf16[128,32]{0,1:T(8,128)(2,1)S(1)} %multiply_convert_fusion.2), channel_id=1, replica_groups=mesh['dp'=16,'tensor'=16] {'tensor'}, dimensions={1}, use_global_device_ids=true | all-gather | bytes 139264 | tf_op jit(solution)/shard_map/all_gather | solution.py:21
  28.8 2.0 convolution_convert_fusion.3
  30.7 0.0 all-gather.11.cloned.1.call-start
  30.8 2.0 convolution_convert_fusion.2
  32.8 0.0 all-gather.7.cloned.1.call-start
  32.8 0.7 all-gather.7.cloned.1.call-update
  33.6 1.2 dynamic_slice.11
  34.8 0.6 fusion.29
  35.5 45.3 %all-gather.9.cloned.1.call-done = bf16[128,8192]{1,0:T(8,128)(2,1)} async-done(((bf16[128,512]{1,0:T(8,128)(2,1)}), bf16[128,8192]{1,0:T(8,128)(2,1)}) %all-gather.9.cloned.1.call-update) | async-done | bytes 2097168 | tf_op jit(solution)/shard_map/all_gather | solution.py:37
  80.7 2.6 fusion.4
  83.3 51.8 %all-gather.11.cloned.1.call-done = bf16[128,8192]{1,0:T(8,128)(2,1)} async-done(((bf16[128,512]{1,0:T(8,128)(2,1)}), bf16[128,8192]{1,0:T(8,128)(2,1)}) %all-gather.11.cloned.1.call-update) | async-done | bytes 2097168 | tf_op jit(solution)/shard_map/all_gather | solution.py:38
  135.2 2.6 fusion.1
  137.8 0.2 convolution_bitcast_fusion
  138.0 54.6 %all-gather.7.cloned.1.call-done = bf16[512,8192]{1,0:T(8,128)(2,1)} async-done(((bf16[32,8192]{1,0:T(8,128)(2,1)}), bf16[512,8192]{1,0:T(8,128)(2,1)}) %all-gather.7.cloned.1.call-update) | async-done | bytes 8388624 | tf_op jit(solution)/shard_map/all_gather | solution.py:48
  192.6 1.3 convolution_bitcast_fusion.1
  193.9 46.9 %all-reduce.2 = (bf16[1,512,16]{1,2,0:T(8,128)(2,1)S(1)}, bf16[1,512,16]{1,2,0:T(8,128)(2,1)S(1)}) all-reduce(f32[1,512,16]{1,2,0:T(8,128)S(1)} %convolution_bitcast_fusion.1, f32[1,512,16]{1,2,0:T(8,128)S(1)} %convolution_bitcast_fusion), channel_id=1, replica_groups=mesh['dp'=16,'tensor'=16] {'tensor'}, use_global_device_ids=true, to_apply=%region_0.1 | all-reduce | flops 16384 | bytes 98304 | tf_op jit(solution)/shard_map/psum | solution.py:58
  240.8 0.2 fusion.13
  240.9 1.2 fusion.11
  242.2 3.5 multiply_convert_fusion
  245.7 0.0 reduce-scatter.12.cloned.1.call-start
  245.7 0.5 reduce-scatter.12.cloned.1.call-update
  246.3 11.6 %fusion.36 = f32[512,8192]{1,0:T(8,128)} fusion(bf16[512,512]{1,0:T(8,128)(2,1)S(1)} %copy-done, bf16[8192,512]{1,0:T(8,128)(2,1)} %param.9), kind=kOutput, calls=%fused_computation.52 | convolution fusion | flops 4294967296 | bytes 25690112 | tf_op jit(solution)/shard_map/dot_general | solution.py:71
  257.9 14.9 %all-gather.2 = bf16[16,8192]{1,0:T(8,128)(2,1)S(1)} all-gather(bf16[16,512]{1,0:T(8,128)(2,1)S(1)} %bitcast.73), channel_id=4, replica_groups=mesh['dp'=16,'tensor'=16] {'tensor'}, dimensions={1}, use_global_device_ids=true | all-gather | bytes 278528 | tf_op jit(solution)/shard_map/all_gather | solution.py:78
  272.8 9.5 %fusion.35 = f32[512,512]{1,0:T(8,128)S(1)} fusion(bf16[512,8192]{1,0:T(8,128)(2,1)} %all-gather.7.cloned.1.call-done, bf16[8192,512]{1,0:T(8,128)(2,1)} %param.9), kind=kOutput, calls=%fused_computation.51 | convolution fusion | flops 4294967296 | bytes 17825792 | tf_op jit(solution)/shard_map/dot_general | solution.py:54
  282.3 1.1 fusion.7
  283.4 42.0 %reduce-scatter.10.cloned.1.call-done = bf16[128,1,512]{2,0,1:T(8,128)(2,1)} async-done(((bf16[128,16,512]{2,0,1:T(8,128)(2,1)}), bf16[128,1,512]{2,0,1:T(8,128)(2,1)}) %reduce-scatter.10.cloned.1.call-update) | async-done | bytes 131088
  325.4 2.0 fusion.8
  327.4 81.0 %reduce-scatter.12.cloned.1.call-done = bf16[128,1,512]{2,0,1:T(8,128)(2,1)} async-done(((bf16[128,16,512]{2,0,1:T(8,128)(2,1)}), bf16[128,1,512]{2,0,1:T(8,128)(2,1)}) %reduce-scatter.12.cloned.1.call-update) | async-done | bytes 131088
  408.5 2.0 fusion.9
  410.4 100.7 %reduce-scatter.8.cloned.1.call-done = f32[32,8192]{1,0:T(8,128)} async-done(((f32[512,8192]{1,0:T(8,128)}), f32[32,8192]{1,0:T(8,128)}) %reduce-scatter.8.cloned.1.call-update) | async-done | bytes 1048592 | tf_op jit(solution)/shard_map/reduce_scatter | solution.py:70
  511.1 2.4 fusion
  (10 shorter events, 0.2 us)
Async XLA Ops:
  7.2 130.6 %copy-start = (bf16[512,512]{1,0:T(8,128)(2,1)S(1)}, bf16[512,512]{1,0:T(8,128)(2,1)}, u32[]{:S(2)}) copy-start(bf16[512,512]{1,0:T(8,128)(2,1)} %param.10) | copy-start | bytes 1572868
  7.2 73.5 %all-gather.9.cloned.1.call-start = ((), (), s32[]{:S(2)}) async-start(), calls=%async_computation.5 | async-start | bytes 2228224 | tf_op jit(solution)/shard_map/all_gather | solution.py:37
  30.7 104.4 %all-gather.11.cloned.1.call-start = ((), (), s32[]{:S(2)}) async-start(), calls=%async_computation.6 | async-start | bytes 2228224 | tf_op jit(solution)/shard_map/all_gather | solution.py:38
  32.8 159.8 %all-gather.7.cloned.1.call-start = ((), (), s32[]{:S(2)}) async-start(), calls=%async_computation.3 | async-start | bytes 8912896 | tf_op jit(solution)/shard_map/all_gather | solution.py:48
  33.5 291.9 %reduce-scatter.10.cloned.1.call-start = ((), (), s32[]{:S(2)}) async-start(), calls=%async_computation.7 | async-start | bytes 2228224
  245.7 162.8 %reduce-scatter.12.cloned.1.call-start = ((), (), s32[]{:S(2)}) async-start(), calls=%async_computation.8 | async-start | bytes 2228224
  246.3 264.9 %reduce-scatter.8.cloned.1.call-start = ((), (), s32[]{:S(2)}) async-start(), calls=%async_computation.4 | async-start | bytes 17825792 | tf_op jit(solution)/shard_map/reduce_scatter | solution.py:70
Sparse Core Ops, SparseCore 0:
  30.9 49.8 all-gather.8
  83.7 51.4 all-gather.10
  137.0 55.5 all-gather.6
  245.8 79.6 reduce-scatter.9
  328.8 79.5 reduce-scatter.11
  410.9 100.2 reduce-scatter.7
where the time goes:
time: 521 us; the launch traced here: 520 us
  waiting for transfers between devices  377 us (72%)
  blocking collectives  82.1 us (16%)
  matrix products  41.8 us (8%)
  between operations  14.2 us (3%)
    unnamed x8, waiting for transfers between devices  124 us
    reduce_scatter x1, waiting for transfers between devices, local(): lax.psum_scatter(lax.dot_general(cotangent, w_query, (((1,), (1,)), ((),...  101 us
    all_gather x1, waiting for transfers between devices, local(): whole = lax.all_gather(tokens, 'tensor', axis=0, tiled=True)  54.6 us
    all_gather x1, waiting for transfers between devices, local(): lax.all_gather(gen_b, 'dp', axis=1, tiled=True)  51.8 us
    psum x1, blocking collectives, local(): down_projection = lax.psum(down_portion, 'tensor')  46.9 us
    all_gather x1, waiting for transfers between devices, local(): lax.all_gather(gen_a, 'dp', axis=1, tiled=True)  45.3 us
    all_gather x1, blocking collectives, local(): hidden = lax.all_gather(hid_part, 'tensor', axis=1, tiled=True)  20.3 us
    all_gather x1, blocking collectives, local(): full_a = lax.all_gather(adapter_down_weight, 'tensor', axis=2, tiled=True)  14.9 us
  transfers between devices with their start and end apart: 6, of which 6 were waited for; matrix products, arithmetic and copies ran while one was open for 7% of the time, Pallas kernels for 0%

commit v1 on v0

--- a/solution.py
+++ b/solution.py
@@ -55,7 +55,11 @@
     down_portion = jnp.einsum(
         "grs,gps->grp", input_columns, adapter_down_weight, preferred_element_type=single_float
     )
-    down_projection = lax.psum(down_portion, "tensor")
+    down_projection = down_portion
+    for hop in (1, 2, 4, 8):
+        down_projection = down_projection + lax.ppermute(
+            down_projection, "tensor", [(dev, dev ^ hop) for dev in range(16)]
+        )
     down_low_rank = down_projection.astype(brain_half_float)
     low_rank_update = jnp.einsum(
         "elm,emn->eln", down_low_rank, adapter_up_weight, preferred_element_type=single_float

time: 521 us -> 531 us (1.019)
  starting transfers between devices: 0.24 us -> 8.72 us
    ppermute x0 -> x4, starting transfers between devices: none -> 8.48 us  [local(): lax.ppermute(down_projection, 'tensor', [(dev, dev ^ hop) for dev in rang...]
  transfers between devices with their start and end apart: 6 -> 10, of which waited for: 6 -> 8; matrix products, arithmetic and copies ran while one was open for 7% -> 7% of each run, Pallas kernels for 0% -> 0%
where the time goes in v1:
time: 531 us
  waiting for transfers between devices  380 us (72%)
  blocking collectives  80.9 us (15%)
  matrix products  41.8 us (8%)
  between operations  14.2 us (3%)
  starting transfers between devices  8.72 us (2%)
    unnamed x8, waiting for transfers between devices  123 us
    reduce_scatter x1, waiting for transfers between devices, local(): lax.psum_scatter(lax.dot_general(cotangent, w_query, (((1,), (1,)), ((),...  101 us
    all_gather x1, waiting for transfers between devices, local(): whole = lax.all_gather(tokens, 'tensor', axis=0, tiled=True)  54.8 us
    all_gather x1, waiting for transfers between devices, local(): lax.all_gather(gen_b, 'dp', axis=1, tiled=True)  51.8 us
    psum x1, blocking collectives, local(): backward_input = lax.psum(backward_portion, 'tensor')  45.7 us
    all_gather x1, waiting for transfers between devices, local(): lax.all_gather(gen_a, 'dp', axis=1, tiled=True)  45.2 us
    all_gather x1, blocking collectives, local(): hidden = lax.all_gather(hid_part, 'tensor', axis=1, tiled=True)  20.3 us
    all_gather x1, blocking collectives, local(): full_a = lax.all_gather(adapter_down_weight, 'tensor', axis=2, tiled=True)  14.9 us
  transfers between devices with their start and end apart: 10, of which 8 were waited for; matrix products, arithmetic and copies ran while one was open for 7% of the time, Pallas kernels for 0%

profile of v1, /device:TPU:2, one launch (start us, length us, event | category | flops | bytes accessed | tf_op | source)
XLA Modules:
  0.0 530.9 jit_solution(4641952495723837595)
XLA Ops:
  7.2 1.2 multiply_convert_fusion.2
  8.4 20.3 %all_gather.16 = bf16[128,512]{0,1:T(8,128)(2,1)S(1)} all-gather(bf16[128,32]{0,1:T(8,128)(2,1)S(1)} %multiply_convert_fusion.2), channel_id=1, replica_groups=mesh['dp'=16,'tensor'=16] {'tensor'}, dimensions={1}, use_global_device_ids=true | all-gather | bytes 139264 | tf_op jit(solution)/shard_map/all_gather | solution.py:21
  28.8 2.0 convolution_convert_fusion.3
  30.8 0.7 all-gather.7.cloned.1.call-update
  31.5 2.0 convolution_convert_fusion.2
  33.6 1.2 dynamic_slice.11
  34.8 0.6 fusion.26
  35.5 45.2 %all-gather.9.cloned.1.call-done = bf16[128,8192]{1,0:T(8,128)(2,1)} async-done(((bf16[128,512]{1,0:T(8,128)(2,1)}), bf16[128,8192]{1,0:T(8,128)(2,1)}) %all-gather.9.cloned.1.call-update) | async-done | bytes 2097168 | tf_op jit(solution)/shard_map/all_gather | solution.py:37
  80.7 2.6 fusion.4
  83.3 54.8 %all-gather.7.cloned.1.call-done = bf16[512,8192]{1,0:T(8,128)(2,1)} async-done(((bf16[32,8192]{1,0:T(8,128)(2,1)}), bf16[512,8192]{1,0:T(8,128)(2,1)}) %all-gather.7.cloned.1.call-update) | async-done | bytes 8388624 | tf_op jit(solution)/shard_map/all_gather | solution.py:48
  138.1 1.3 convolution_bitcast_fusion.1
  139.7 51.8 %all-gather.11.cloned.1.call-done = bf16[128,8192]{1,0:T(8,128)(2,1)} async-done(((bf16[128,512]{1,0:T(8,128)(2,1)}), bf16[128,8192]{1,0:T(8,128)(2,1)}) %all-gather.11.cloned.1.call-update) | async-done | bytes 2097168 | tf_op jit(solution)/shard_map/all_gather | solution.py:38
  191.4 2.6 fusion.1
  194.1 1.6 collective-permute-start.1
  195.9 2.1 collective-permute-done.1
  198.1 2.6 collective-permute-start.2
  200.7 45.7 %psum.7 = bf16[1,512,16]{1,2,0:T(8,128)(2,1)S(1)} all-reduce(f32[1,512,16]{1,2,0:T(8,128)S(1)} %convolution_bitcast_fusion), channel_id=1, replica_groups=mesh['dp'=16,'tensor'=16] {'tensor'}, use_global_device_ids=true, to_apply=%region_1.2 | all-reduce | flops 8192 | bytes 49152 | tf_op jit(solution)/shard_map/psum | solution.py:72
  246.4 4.0 collective-permute-start.3
  250.4 1.2 fusion.11
  251.6 2.7 collective-permute-done.3
  254.5 3.5 multiply_convert_fusion
  258.1 0.5 reduce-scatter.12.cloned.1.call-update
  258.6 11.6 %fusion.33 = f32[512,8192]{1,0:T(8,128)} fusion(bf16[512,512]{1,0:T(8,128)(2,1)S(1)} %copy-done, bf16[8192,512]{1,0:T(8,128)(2,1)} %param.9), kind=kOutput, calls=%fused_computation.50 | convolution fusion | flops 4294967296 | bytes 25690112 | tf_op jit(solution)/shard_map/dot_general | solution.py:75
  270.3 14.9 %all-gather.2 = bf16[16,8192]{1,0:T(8,128)(2,1)S(1)} all-gather(bf16[16,512]{1,0:T(8,128)(2,1)S(1)} %bitcast.72), channel_id=4, replica_groups=mesh['dp'=16,'tensor'=16] {'tensor'}, dimensions={1}, use_global_device_ids=true | all-gather | bytes 278528 | tf_op jit(solution)/shard_map/all_gather | solution.py:82
  285.2 9.5 %fusion.32 = f32[512,512]{1,0:T(8,128)S(1)} fusion(bf16[512,8192]{1,0:T(8,128)(2,1)} %all-gather.7.cloned.1.call-done, bf16[8192,512]{1,0:T(8,128)(2,1)} %param.9), kind=kOutput, calls=%fused_computation.49 | convolution fusion | flops 4294967296 | bytes 17825792 | tf_op jit(solution)/shard_map/dot_general | solution.py:54
  294.7 1.1 fusion.7
  295.8 40.2 %reduce-scatter.10.cloned.1.call-done = bf16[128,1,512]{2,0,1:T(8,128)(2,1)} async-done(((bf16[128,16,512]{2,0,1:T(8,128)(2,1)}), bf16[128,1,512]{2,0,1:T(8,128)(2,1)}) %reduce-scatter.10.cloned.1.call-update) | async-done | bytes 131088
  336.0 2.0 fusion.8
  337.9 81.1 %reduce-scatter.12.cloned.1.call-done = bf16[128,1,512]{2,0,1:T(8,128)(2,1)} async-done(((bf16[128,16,512]{2,0,1:T(8,128)(2,1)}), bf16[128,1,512]{2,0,1:T(8,128)(2,1)}) %reduce-scatter.12.cloned.1.call-update) | async-done | bytes 131088
  419.0 2.0 fusion.9
  421.0 100.7 %reduce-scatter.8.cloned.1.call-done = f32[32,8192]{1,0:T(8,128)} async-done(((f32[512,8192]{1,0:T(8,128)}), f32[32,8192]{1,0:T(8,128)}) %reduce-scatter.8.cloned.1.call-update) | async-done | bytes 1048592 | tf_op jit(solution)/shard_map/reduce_scatter | solution.py:74
  521.7 2.4 fusion
  (22 shorter events, 1.0 us)
Async XLA Ops:
  7.2 188.5 %copy-start = (bf16[512,512]{1,0:T(8,128)(2,1)S(1)}, bf16[512,512]{1,0:T(8,128)(2,1)}, u32[]{:S(2)}) copy-start(bf16[512,512]{1,0:T(8,128)(2,1)} %param.10) | copy-start | bytes 1572868
  7.2 73.5 %all-gather.9.cloned.1.call-start = ((), (), s32[]{:S(2)}) async-start(), calls=%async_computation.5 | async-start | bytes 2228224 | tf_op jit(solution)/shard_map/all_gather | solution.py:37
  30.7 107.4 %all-gather.7.cloned.1.call-start = ((), (), s32[]{:S(2)}) async-start(), calls=%async_computation.3 | async-start | bytes 8912896 | tf_op jit(solution)/shard_map/all_gather | solution.py:48
  31.5 159.9 %all-gather.11.cloned.1.call-start = ((), (), s32[]{:S(2)}) async-start(), calls=%async_computation.6 | async-start | bytes 2228224 | tf_op jit(solution)/shard_map/all_gather | solution.py:38
  33.5 302.4 %reduce-scatter.10.cloned.1.call-start = ((), (), s32[]{:S(2)}) async-start(), calls=%async_computation.7 | async-start | bytes 2228224
  139.4 54.6 %collective-permute-start = (f32[1,512,16]{1,2,0:T(8,128)S(1)}, f32[1,512,16]{1,2,0:T(8,128)S(1)}, u32[]{:S(2)}, u32[]{:S(2)}) collective-permute-start(f32[1,512,16]{1,2,0:T(8,128)S(1)} %convolution_bitcast_fusion.1), channel_id=1, source_target_pairs={{0,1},{1,0},{2,3},{3,2},{4,5},{5,4},{6,7},{7,6},{8,9},{9,8},{10,11... | collective-permute-start | bytes 98312 | tf_op jit(solution)/shard_map/ppermute | solution.py:60
  194.1 4.0 collective-permute-start.1
  198.1 48.4 %collective-permute-start.2 = (f32[1,512,16]{1,2,0:T(8,128)S(1)}, f32[1,512,16]{1,2,0:T(8,128)S(1)}, u32[]{:S(2)}, u32[]{:S(2)}) collective-permute-start(f32[1,512,16]{1,2,0:T(8,128)S(1)} %add.46), channel_id=1, source_target_pairs={{0,4},{1,5},{2,6},{3,7},{4,0},{5,1},{6,2},{7,3},{8,12},{9,13},{10,... | collective-permute-start | bytes 98312 | tf_op jit(solution)/shard_map/ppermute | solution.py:60
  246.4 7.9 %collective-permute-start.3 = (f32[1,512,16]{1,2,0:T(8,128)S(1)}, f32[1,512,16]{1,2,0:T(8,128)S(1)}, u32[]{:S(2)}, u32[]{:S(2)}) collective-permute-start(f32[1,512,16]{1,2,0:T(8,128)S(1)} %add.47), channel_id=1, source_target_pairs={{0,8},{1,9},{2,10},{3,11},{4,12},{5,13},{6,14},{7,15},{8,0},{9,1},... | collective-permute-start | bytes 98312 | tf_op jit(solution)/shard_map/ppermute | solution.py:60
  258.0 161.0 %reduce-scatter.12.cloned.1.call-start = ((), (), s32[]{:S(2)}) async-start(), calls=%async_computation.8 | async-start | bytes 2228224
  258.6 263.1 %reduce-scatter.8.cloned.1.call-start = ((), (), s32[]{:S(2)}) async-start(), calls=%async_computation.4 | async-start | bytes 17825792 | tf_op jit(solution)/shard_map/reduce_scatter | solution.py:74
Sparse Core Ops, SparseCore 0:
  30.9 49.8 all-gather.8
  82.5 55.5 all-gather.6
  141.1 50.2 all-gather.10
  258.1 77.7 reduce-scatter.9
  339.4 79.6 reduce-scatter.11
  421.4 100.2 reduce-scatter.7
